TPU v7x, 32 devices: a whole 2x2x4 slice. The times are simulated.
32 devices in a mesh: grp: 2 (over x), ctx: 16 (over z, y, core).
Axes of the slice: x: 2, y: 2, z: 4, core: 2. Of those that a mesh axis runs over, the one named last changes fastest.
Arguments:
- queries: bfloat16 [960, 4096], P(None, ('grp', 'ctx')), parts along dimension 1, may hold values from -6 to 6
- key_rows: bfloat16 [960, 4096], P(None, ('grp', 'ctx')), parts along dimension 1, may hold values from -6 to 6
- value_rows: bfloat16 [960, 4096], P(None, ('grp', 'ctx')), parts along dimension 1, may hold values from -6 to 6
- short_taps: float32 [3, 960, 7], replicated, may hold values from -2 to 2
- long_filter: bfloat16 [960, 2048], P('ctx'), may hold values from -0.125 to 0.125
Outputs:
- mixed: bfloat16 [960, 4096], P(None, ('grp', 'ctx')), parts along dimension 1
There are 2 independent parts, one for each index of `grp`. A program takes and returns all parts, laid end to end along the dimension named above; an argument that names none is the same for every part. Nothing has to cross between parts.
All inputs are finite; a program needn't handle non-finite values.
Results may differ from a plain program's by a relative error of at most 0.0057.
Values may be sent and summed in bfloat16 or wider, within the bound.
A program may use at most 64 MiB of HBM per device.

v0:
```python
import math
import jax
import jax.numpy as jnp
from jax import lax
from jax.sharding import PartitionSpec as P

TAPS = 7
precise = lax.Precision.HIGH


def with_halo(value, sides, width):
    for axis, dim in sides:
        size, length = (lax.axis_size(axis), value.shape[dim])
        up = [(i, (i + 1) % size) for i in range(size - 1)]
        down = [(j, i) for i, j in up]
        last = lax.slice_in_dim(value, length - width, length, axis=dim)
        leading = lax.slice_in_dim(value, 0, width, axis=dim)
        before = lax.ppermute(last, axis, up)
        after = lax.ppermute(leading, axis, down)
        value = jnp.concatenate([before, value, after], axis=dim)
    return value


def angles(count_rows, count_cols, modulus):
    row_ids = lax.broadcasted_iota(jnp.int32, (count_rows, count_cols), 0)
    col_ids = lax.broadcasted_iota(jnp.int32, (count_rows, count_cols), 1)
    phase = (row_ids * col_ids % modulus).astype(jnp.float32) * (2.0 * math.pi / modulus)
    return (jnp.cos(phase), jnp.sin(phase))


def fourier_tables(length):
    inner_len = min(128, length)
    padded_len = 2 * length
    outer_len = padded_len // inner_len
    cos_outer, sin_outer = angles(outer_len // 2, outer_len, outer_len)
    cos_twist, sin_twist = angles(outer_len, inner_len, padded_len)
    cos_inner, sin_inner = angles(inner_len, inner_len, inner_len)
    outer_fwd = jnp.stack([cos_outer, -sin_outer])
    inner_fwd = jnp.stack([jnp.stack([cos_inner, -sin_inner]), jnp.stack([sin_inner, cos_inner])])
    inner_inv = jnp.stack([jnp.stack([cos_inner, sin_inner]), jnp.stack([-sin_inner, cos_inner])])
    return (outer_fwd, cos_twist, sin_twist, inner_fwd, inner_inv, padded_len)


def forward(signal, tables):
    outer_fwd, cos_twist, sin_twist, inner_fwd, inner_inv, padded_len = tables
    shaped = signal.reshape(signal.shape[:-1] + (outer_fwd.shape[1], inner_fwd.shape[2]))
    first = jnp.einsum("...ab,caf->...cfb", shaped, outer_fwd, precision=precise)
    first_real = first[..., 0, :, :]
    first_imag = first[..., 1, :, :]
    twist = jnp.stack(
        [
            first_real * cos_twist + first_imag * sin_twist,
            first_imag * cos_twist - first_real * sin_twist,
        ],
        axis=-3,
    )
    return jnp.einsum("...cfb,cdbk->...dfk", twist, inner_fwd, precision=precise)


def inverse(spectrum, tables):
    outer_fwd, cos_twist, sin_twist, inner_fwd, inner_inv, padded_len = tables
    first = jnp.einsum("...cfk,cdkb->...dfb", spectrum, inner_inv, precision=precise)
    first_real = first[..., 0, :, :]
    first_imag = first[..., 1, :, :]
    twist = jnp.stack(
        [
            first_real * cos_twist - first_imag * sin_twist,
            first_imag * cos_twist + first_real * sin_twist,
        ],
        axis=-3,
    )
    result = jnp.einsum("...cfb,caf->...ab", twist, outer_fwd, precision=precise)
    result = result / padded_len
    return result.reshape(result.shape[:-2] + (result.shape[-2] * result.shape[-1],))


def on_device(queries, key_rows, value_rows, short_taps, long_filter):
    tokens = queries.shape[1]
    rim_width = TAPS - 1
    stacked = jnp.stack([queries, key_rows, value_rows])
    padded = with_halo(stacked, (("ctx", 2),), rim_width)
    mirrored_taps = short_taps[:, ::-1, :]
    causal = jnp.zeros(stacked.shape, jnp.float32)
    anticausal = jnp.zeros(stacked.shape, jnp.float32)
    for offset in range(TAPS):
        begin = rim_width - offset
        causal = causal + short_taps[:, :, offset, None] * padded[:, :, begin : begin + tokens]
        later = rim_width + offset
        anticausal = (
            anticausal + mirrored_taps[:, :, offset, None] * padded[:, :, later : later + tokens]
        )
    product_a = (causal[1] * causal[2]).astype(jnp.bfloat16)
    product_b = (anticausal[1] * anticausal[2]).astype(jnp.bfloat16)
    tables = fourier_tables(long_filter.shape[1])
    outgoing = jnp.stack([product_a, product_b[::-1]])
    channel_rows = lax.all_to_all(outgoing, "ctx", split_axis=1, concat_axis=2, tiled=True)
    filter_spec = forward(long_filter.astype(jnp.float32), tables)
    data_spec = forward(channel_rows.astype(jnp.float32), tables)
    filter_real = filter_spec[:, 0]
    filter_imag = filter_spec[:, 1]
    data_real = data_spec[:, :, 0]
    data_imag = data_spec[:, :, 1]
    first_real = filter_real * data_real[0] - filter_imag * data_imag[0]
    first_imag = filter_real * data_imag[0] + filter_imag * data_real[0]
    second_real = filter_real * data_real[1] + filter_imag * data_imag[1]
    second_imag = filter_real * data_imag[1] - filter_imag * data_real[1]
    spectrum = jnp.stack(
        [jnp.stack([first_real, first_imag], axis=1), jnp.stack([second_real, second_imag], axis=1)]
    )
    convolved = inverse(spectrum, tables).astype(jnp.bfloat16)
    token_rows = lax.all_to_all(convolved, "ctx", split_axis=2, concat_axis=1, tiled=True)
    mixed_b = token_rows[1][::-1]
    result = causal[0] * token_rows[0].astype(jnp.float32) + anticausal[0] * mixed_b.astype(
        jnp.float32
    )
    return result.astype(jnp.bfloat16)


def solution(mesh):
    placed = (
        P(None, ("grp", "ctx")),
        P(None, ("grp", "ctx")),
        P(None, ("grp", "ctx")),
        P(),
        P("ctx", None),
    )
    return jax.shard_map(
        on_device, mesh=mesh, in_specs=placed, out_specs=P(None, ("grp", "ctx")), check_vma=False
    )
```

profile of v0, /device:TPU:0, one launch (start us, length us, event | category | flops | bytes accessed | tf_op | source)
XLA Modules:
  0.0 102.4 jit_solution(13261690223920789769)
XLA Ops:
  0.0 1.3 %pad_maximum_fusion.2 = bf16[3,960,128]{2,1,0:T(8,128)(2,1)S(1)} fusion(bf16[1,960,128]{2,1,0:T(8,128)(2,1)} %bitcast.184, bf16[1,960,128]{2,1,0:T(8,128)(2,1)} %bitcast.188, bf16[1,960,128]{2,1,0:T(8,128)(2,1)} %bitcast.192), kind=kLoop, calls=%fused_computation.55 | loop fusion | flops 737280 | bytes 1474560 | tf_op jit(solution)/shard_map/stack | solution.py:80
  1.9 1.3 %collective-permute-start.1 = (bf16[3,960,6]{1,2,0:T(8,128)(2,1)S(1)}, bf16[3,960,6]{1,2,0:T(8,128)(2,1)S(1)}, u32[]{:S(2)}, u32[]{:S(2)}) collective-permute-start(bf16[3,960,6]{1,2,0:T(8,128)(2,1)S(1)} %copy.51), channel_id=1, source_target_pairs={{1,0},{2,1},{3,2},{4,3},{5,4},{6,5},{7,6},{8,7},{9,8},{10,9},{11,1... | collective-permute-start | bytes 103688 | tf_op jit(solution)/shard_map/ppermute | solution.py:19
  3.5 3.0 %collective-permute-start = (bf16[3,960,6]{1,2,0:T(8,128)(2,1)S(1)}, bf16[3,960,6]{1,2,0:T(8,128)(2,1)S(1)}, u32[]{:S(2)}, u32[]{:S(2)}) collective-permute-start(bf16[3,960,6]{1,2,0:T(8,128)(2,1)S(1)} %copy.47), channel_id=1, source_target_pairs={{0,1},{1,2},{2,3},{3,4},{4,5},{5,6},{6,7},{7,8},{8,9},{9,10},{10,1... | collective-permute-start | bytes 103688 | tf_op jit(solution)/shard_map/ppermute | solution.py:18
  7.3 0.7 reverse.8
  8.1 0.7 reverse.7
  9.0 0.7 reverse.12
  10.4 0.7 reverse.11
  11.2 0.7 reverse.10
  15.4 0.7 fusion.60
  16.7 0.7 reverse.13
  18.7 1.2 %copy.52 = bf16[3,960,6]{2,1,0:T(8,128)(2,1)} copy(bf16[3,960,6]{1,2,0:T(8,128)(2,1)S(1)} %collective-permute-done.1) | data formatting | bytes 69120 | tf_op jit(solution)/shard_map/ppermute | solution.py:19
  19.9 2.5 %maximum_maximum_fusion = (bf16[3,960,134]{2,1,0:T(8,128)(2,1)S(1)}, bf16[3,960,134]{2,1,0:T(8,128)(2,1)S(1)}) fusion(bf16[1,960,128]{2,1,0:T(8,128)(2,1)S(1)} %bitcast.185, bf16[1,960,128]{2,1,0:T(8,128)(2,1)S(1)} %bitcast.189, bf16[1,960,128]{2,1,0:T(8,128)(2,1)S(1)} %bitcast.193, bf16[3,960,6]{2,1,0:T(8,128)(2,1)S(1)} %copy.48, bf16[3,960,6]{2,1,0:T(8,128)(2,1)} %copy.52), kind=kLoop, calls=%fused_computation.39 | loop fusion | flops 6174720 | bytes 2350080 | tf_op jit(solution)/shard_map/concatenate | solution.py:20
  22.6 4.5 %fusion.31 = f32[3,960,128]{2,1,0:T(8,128)S(1)} fusion(bf16[3,960,134]{2,1,0:T(8,128)(2,1)S(1)} %get-tuple-element.16, f32[3,960]{1,0:T(4,128)S(1)} %copy-done.13, f32[3,960]{1,0:T(4,128)S(1)} %copy-done.14, f32[3,960]{1,0:T(4,128)S(1)} %copy-done.17, f32[3,960]{1,0:T(4,128)S(1)} %copy-done.18, f32[3,960]{1,0:T(4,128)S(1)} %copy-done.15, ...), kind=kLoop, calls=%fused_computation.38 | loop fusion | flops 8110080 | bytes 6716160 | tf_op jit(solution)/shard_map/add | solution.py:90
  27.1 1.1 %copy-done = f32[3,960,128]{2,1,0:T(8,128)} copy-done((f32[3,960,128]{2,1,0:T(8,128)}, f32[3,960,128]{2,1,0:T(8,128)S(1)}, u32[]{:S(2)}) %copy-start) | copy-done | bytes 1474584
  29.0 4.3 %fusion.25 = f32[3,960,128]{2,1,0:T(8,128)S(1)} fusion(bf16[3,960,134]{2,1,0:T(8,128)(2,1)S(1)} %get-tuple-element.15, f32[3,960]{1,0:T(4,128)S(1)} %get-tuple-element.34, f32[3,960]{1,0:T(4,128)S(1)} %get-tuple-element.35, f32[3,960]{1,0:T(4,128)S(1)} %copy-done.11, f32[3,960]{1,0:T(4,128)S(1)} %copy-done.12, f32[3,960]{1,0:T(4,128)S(1)} %copy-done.9, ...), kind=kLoop, calls=%fused_computation.32 | loop fusion | flops 8110080 | bytes 6716160 | tf_op jit(solution)/shard_map/add | solution.py:87
  33.3 1.1 %copy-done.1 = f32[3,960,128]{2,1,0:T(8,128)} copy-done((f32[3,960,128]{2,1,0:T(8,128)}, f32[3,960,128]{2,1,0:T(8,128)S(1)}, u32[]{:S(2)}) %copy-start.1) | copy-done | bytes 1474584
  34.5 1.3 %copy.53 = bf16[2,960,128]{2,0,1:T(2,128)(2,1)} copy(bf16[2,960,128]{2,1,0:T(8,128)(2,1)S(1)} %pad_maximum_fusion.3) | data formatting | bytes 983040 | tf_op jit(solution)/shard_map/stack | solution.py:95
  35.8 8.1 %all-to-all-start = ((bf16[2,960,128]{2,0,1:T(2,128)(2,1)}), bf16[2,960,128]{2,0,1:T(2,128)(2,1)S(1)}, u32[]{:S(2)}, u32[]{:S(2)}) async-start(bf16[2,960,128]{2,0,1:T(2,128)(2,1)} %copy.53), calls=%async_computation | async-start | bytes 983040 | tf_op jit(solution)/shard_map/all_to_all | solution.py:96
  45.2 2.0 %fusion.17 = f32[60,2,32,128]{3,0,2,1:T(8,128)S(1)} fusion(f32[60,2,32,128]{3,2,0,1:T(8,128)S(1)} %pad_maximum_fusion, f32[1,2,128,128]{3,2,0,1:T(8,128)S(1)} %get-tuple-element.22, f32[1,2,128,128]{3,2,0,1:T(8,128)S(1)} %get-tuple-element.32), kind=kOutput, calls=%fused_computation.25 | convolution fusion | flops 755040256 | bytes 4194304 | tf_op jit(solution)/shard_map/...cfb,cdbk->...dfk/dot_general | solution.py:57
  47.2 10.4 %all-to-all-done = bf16[2,960,128]{2,0,1:T(2,128)(2,1)S(1)} async-done(((bf16[2,960,128]{2,0,1:T(2,128)(2,1)}), bf16[2,960,128]{2,0,1:T(2,128)(2,1)S(1)}, u32[]{:S(2)}, u32[]{:S(2)}) %all-to-all-start) | async-done | bytes 491552 | tf_op jit(solution)/shard_map/all_to_all | solution.py:96
  57.6 1.2 %convolution_bitcast_fusion = f32[2,60,2,32,128]{4,3,1,0,2:T(8,128)S(1)} fusion(bf16[2,16,60,128]{3,0,2,1:T(2,128)(2,1)S(1)} %bitcast.196, f32[1,16,32]{2,1,0:T(8,128)S(1)} %get-tuple-element.46, f32[1,16,32]{2,1,0:T(8,128)S(1)} %get-tuple-element.47), kind=kOutput, calls=%fused_computation.17 | convolution fusion | flops 94372864 | bytes 4427776 | tf_op jit(solution)/shard_map/...ab,caf->...cfb/dot_general | solution.py:47
  58.8 0.8 multiply_add_fusion.1
  60.0 5.0 %fusion.8 = f32[2,60,2,32,128]{4,1,3,2,0:T(8,128)S(1)} fusion(f32[2,60,2,32,128,1]{4,3,1,0,2,5:T(8,128)S(1)} %maximum_bitcast_fusion.1, f32[1,2,128,128]{3,2,0,1:T(8,128)S(1)} %get-tuple-element.22, f32[1,2,128,128]{3,2,0,1:T(8,128)S(1)} %get-tuple-element.32), kind=kOutput, calls=%fused_computation.10 | convolution fusion | flops 1510014976 | bytes 8126464 | tf_op jit(solution)/shard_map/...cfb,cdbk->...dfk/dot_general | solution.py:57
  65.0 1.0 multiply_subtract_fusion.3
  67.3 4.5 %fusion.14 = f32[2,60,2,32,128]{4,3,1,0,2:T(8,128)S(1)} fusion(f32[2,60,2,32,128,1]{4,1,3,2,0,5:T(8,128)S(1)} %maximum_bitcast_fusion, f32[1,2,128,128]{3,2,1,0:T(8,128)S(1)} %copy-done.7, f32[1,2,128,128]{3,2,1,0:T(8,128)S(1)} %copy-done.6), kind=kOutput, calls=%fused_computation.16 | convolution fusion | flops 1510014976 | bytes 8126464 | tf_op jit(solution)/shard_map/...cfk,cdkb->...dfb/dot_general | solution.py:62
  72.4 1.3 %fusion.41 = bf16[2,60,16,128]{3,2,1,0:T(8,128)(2,1)S(1)} fusion(f32[2,60,1,32,128]{4,3,1,0,2:T(8,128)S(1)} %get-tuple-element.10, f32[2,60,1,32,128]{4,3,1,0,2:T(8,128)S(1)} %get-tuple-element.9, f32[1,16,32]{2,1,0:T(8,128)S(1)} %get-tuple-element.46, f32[1,16,32]{2,1,0:T(8,128)S(1)} %get-tuple-element.47), kind=kOutput, calls=%fused_computation.44 | convolution fusion | flops 95847424 | bytes 4427776 | tf_op jit(solution)/shard_map/...cfb,caf->...ab/dot_general | solution.py:72
  73.7 0.8 copy.89
  74.6 2.8 %reshape.225 = bf16[16,2,7680]{2,1,0:T(2,128)(2,1)S(1)} reshape(bf16[2048,2,60]{2,1,0:T(2,128)(2,1)S(1)} %bitcast.182) | data formatting | bytes 983040
  77.4 17.7 %all_to_all.30 = bf16[16,2,7680]{2,1,0:T(2,128)(2,1)S(1)} all-to-all(bf16[16,2,7680]{2,1,0:T(2,128)(2,1)S(1)} %reshape.225), channel_id=1, replica_groups=mesh['grp'=2,'ctx'=16] {'ctx'}, dimensions={0} | all-to-all | bytes 983040 | tf_op jit(solution)/shard_map/all_to_all | solution.py:111
  95.0 3.5 %reshape.226 = bf16[2048,2,60]{2,1,0:T(2,128)(2,1)S(1)} reshape(bf16[16,2,7680]{2,1,0:T(2,128)(2,1)S(1)} %all_to_all.30) | data formatting | bytes 983040
  98.6 0.8 copy.88
  100.4 2.0 %fusion.46 = bf16[960,128]{1,0:T(8,128)(2,1)} fusion(f32[3,960,128]{2,1,0:T(8,128)} %copy-done, f32[960,128]{1,0:T(8,128)S(1)} %reshape.208, f32[3,960,128]{2,1,0:T(8,128)} %copy-done.1, bf16[960,128]{1,0:T(8,128)(2,1)S(1)} %rev.8), kind=kLoop, calls=%fused_computation.59 | loop fusion | flops 614400 | bytes 1966080 | tf_op jit(solution)/shard_map/convert_element_type | solution.py:116
  (86 shorter events, 13.1 us)
Async XLA Ops:
  1.3 5.9 %copy-start.8 = (f32[3,960,7]{1,2,0:T(8,128)S(1)}, f32[3,960,7]{1,2,0:T(8,128)}, u32[]{:S(2)}) copy-start(f32[3,960,7]{1,2,0:T(8,128)} %param.8) | copy-start | bytes 241924
  1.6 16.6 %copy-start.5 = (bf16[60,2048]{1,0:T(8,128)(2,1)S(1)}, bf16[60,2048]{1,0:T(8,128)(2,1)}, u32[]{:S(2)}) copy-start(bf16[60,2048]{1,0:T(8,128)(2,1)} %param.9) | copy-start | bytes 737284
  1.9 16.8 %collective-permute-start.1 = (bf16[3,960,6]{1,2,0:T(8,128)(2,1)S(1)}, bf16[3,960,6]{1,2,0:T(8,128)(2,1)S(1)}, u32[]{:S(2)}, u32[]{:S(2)}) collective-permute-start(bf16[3,960,6]{1,2,0:T(8,128)(2,1)S(1)} %copy.51), channel_id=1, source_target_pairs={{1,0},{2,1},{3,2},{4,3},{5,4},{6,5},{7,6},{8,7},{9,8},{10,9},{11,1... | collective-permute-start | bytes 103688 | tf_op jit(solution)/shard_map/ppermute | solution.py:19
  3.5 14.7 %collective-permute-start = (bf16[3,960,6]{1,2,0:T(8,128)(2,1)S(1)}, bf16[3,960,6]{1,2,0:T(8,128)(2,1)S(1)}, u32[]{:S(2)}, u32[]{:S(2)}) collective-permute-start(bf16[3,960,6]{1,2,0:T(8,128)(2,1)S(1)} %copy.47), channel_id=1, source_target_pairs={{0,1},{1,2},{2,3},{3,4},{4,5},{5,6},{6,7},{7,8},{8,9},{9,10},{10,1... | collective-permute-start | bytes 103688 | tf_op jit(solution)/shard_map/ppermute | solution.py:18
  6.9 13.0 %copy-start.2 = (bf16[960,128]{1,0:T(8,128)(2,1)S(1)}, bf16[960,128]{1,0:T(8,128)(2,1)}, u32[]{:S(2)}) copy-start(bf16[960,128]{1,0:T(8,128)(2,1)} %param.7) | copy-start | bytes 737284
  6.9 13.0 %copy-start.3 = (bf16[960,128]{1,0:T(8,128)(2,1)S(1)}, bf16[960,128]{1,0:T(8,128)(2,1)}, u32[]{:S(2)}) copy-start(bf16[960,128]{1,0:T(8,128)(2,1)} %param.6) | copy-start | bytes 737284
  6.9 13.0 %copy-start.4 = (bf16[960,128]{1,0:T(8,128)(2,1)S(1)}, bf16[960,128]{1,0:T(8,128)(2,1)}, u32[]{:S(2)}) copy-start(bf16[960,128]{1,0:T(8,128)(2,1)} %param.5) | copy-start | bytes 737284
  19.9 2.6 %copy-start.13 = (f32[3,960]{1,0:T(4,128)S(1)}, f32[3,960]{1,0:T(4,128)}, u32[]{:S(2)}) copy-start(f32[3,960]{1,0:T(4,128)} %get-tuple-element.40) | copy-start | bytes 34564
  19.9 2.6 %copy-start.14 = (f32[3,960]{1,0:T(4,128)S(1)}, f32[3,960]{1,0:T(4,128)}, u32[]{:S(2)}) copy-start(f32[3,960]{1,0:T(4,128)} %get-tuple-element.41) | copy-start | bytes 34564
  19.9 2.6 %copy-start.15 = (f32[3,960]{1,0:T(4,128)S(1)}, f32[3,960]{1,0:T(4,128)}, u32[]{:S(2)}) copy-start(f32[3,960]{1,0:T(4,128)} %get-tuple-element.44) | copy-start | bytes 34564
  19.9 2.6 %copy-start.16 = (f32[3,960]{1,0:T(4,128)S(1)}, f32[3,960]{1,0:T(4,128)}, u32[]{:S(2)}) copy-start(f32[3,960]{1,0:T(4,128)} %get-tuple-element.45) | copy-start | bytes 34564
  19.9 2.6 %copy-start.17 = (f32[3,960]{1,0:T(4,128)S(1)}, f32[3,960]{1,0:T(4,128)}, u32[]{:S(2)}) copy-start(f32[3,960]{1,0:T(4,128)} %get-tuple-element.42) | copy-start | bytes 34564
  19.9 2.6 %copy-start.18 = (f32[3,960]{1,0:T(4,128)S(1)}, f32[3,960]{1,0:T(4,128)}, u32[]{:S(2)}) copy-start(f32[3,960]{1,0:T(4,128)} %get-tuple-element.43) | copy-start | bytes 34564
  19.9 2.6 %copy-start.20 = (f32[3,960,1]{1,0,2:T(4,128)S(1)}, f32[3,960,1]{1,0,2:T(4,128)}, u32[]{:S(2)}) copy-start(f32[3,960,1]{1,0,2:T(4,128)} %copy.139) | copy-start | bytes 34564
  22.5 6.4 %copy-start.9 = (f32[3,960]{1,0:T(4,128)S(1)}, f32[3,960]{1,0:T(4,128)}, u32[]{:S(2)}) copy-start(f32[3,960]{1,0:T(4,128)} %get-tuple-element.38) | copy-start | bytes 34564
  22.5 6.4 %copy-start.10 = (f32[3,960]{1,0:T(4,128)S(1)}, f32[3,960]{1,0:T(4,128)}, u32[]{:S(2)}) copy-start(f32[3,960]{1,0:T(4,128)} %get-tuple-element.39) | copy-start | bytes 34564
  22.6 6.4 %copy-start.11 = (f32[3,960]{1,0:T(4,128)S(1)}, f32[3,960]{1,0:T(4,128)}, u32[]{:S(2)}) copy-start(f32[3,960]{1,0:T(4,128)} %get-tuple-element.36) | copy-start | bytes 34564
  22.6 6.4 %copy-start.12 = (f32[3,960]{1,0:T(4,128)S(1)}, f32[3,960]{1,0:T(4,128)}, u32[]{:S(2)}) copy-start(f32[3,960]{1,0:T(4,128)} %get-tuple-element.37) | copy-start | bytes 34564
  22.6 6.4 %copy-start.19 = (f32[3,960,1]{1,0,2:T(4,128)S(1)}, f32[3,960,1]{1,0,2:T(4,128)}, u32[]{:S(2)}) copy-start(f32[3,960,1]{1,0,2:T(4,128)} %copy.140) | copy-start | bytes 34564
  27.1 1.1 %copy-start = (f32[3,960,128]{2,1,0:T(8,128)}, f32[3,960,128]{2,1,0:T(8,128)S(1)}, u32[]{:S(2)}) copy-start(f32[3,960,128]{2,1,0:T(8,128)S(1)} %fusion.31) | copy-start | bytes 4423684
  33.3 1.1 %copy-start.1 = (f32[3,960,128]{2,1,0:T(8,128)}, f32[3,960,128]{2,1,0:T(8,128)S(1)}, u32[]{:S(2)}) copy-start(f32[3,960,128]{2,1,0:T(8,128)S(1)} %fusion.25) | copy-start | bytes 4423684
  35.8 21.7 %all-to-all-start = ((bf16[2,960,128]{2,0,1:T(2,128)(2,1)}), bf16[2,960,128]{2,0,1:T(2,128)(2,1)S(1)}, u32[]{:S(2)}, u32[]{:S(2)}) async-start(bf16[2,960,128]{2,0,1:T(2,128)(2,1)} %copy.53), calls=%async_computation | async-start | bytes 983040 | tf_op jit(solution)/shard_map/all_to_all | solution.py:96
  66.3 0.9 copy-start.6
  66.4 1.0 copy-start.7
where the time goes:
time: 103 us; the launch traced here: 102 us
  local copies, waits for them, and re-layouts  26.3 us (26%)
  other arithmetic  20.2 us (20%)
  blocking collectives  17.7 us (17%)
  matrix products  14.7 us (14%)
  starting transfers between devices  12.5 us (12%)
  waiting for transfers between devices  10.4 us (10%)
    unnamed x67, local copies, waits for them, and re-layouts  19.2 us
    all_to_all x1, blocking collectives, on_device(): lax.all_to_all(convolved, 'ctx', split_axis=2, concat_axis=1, tiled=True)  17.7 us
    all_to_all x1, waiting for transfers between devices, on_device(): lax.all_to_all(outgoing, 'ctx', split_axis=1, concat_axis=2, tiled=True)  10.4 us
    all_to_all x1, starting transfers between devices, on_device(): lax.all_to_all(outgoing, 'ctx', split_axis=1, concat_axis=2, tiled=True)  8.13 us
    dot_general x2, matrix products, forward(): jnp.einsum('...cfb,cdbk->...dfk', twist, inner_fwd, precision=precise)  6.97 us
    add x1, other arithmetic, on_device(): anticausal + mirrored_taps[:, :, offset, None] * padded[:, :, later:later...  4.54 us
    dot_general x1, matrix products, inverse(): jnp.einsum('...cfk,cdkb->...dfb', spectrum, inner_inv, precision=precise)  4.47 us
    add x1, other arithmetic, on_device(): causal + short_taps[:, :, offset, None] * padded[:, :, begin:begin + tokens]  4.31 us
  transfers between devices with their start and end apart: 3, of which 1 were waited for; matrix products, arithmetic and copies ran while one was open for 15% of the time, Pallas kernels for 0%

commit v1 on v0

--- a/solution.py
+++ b/solution.py
@@ -108,7 +108,10 @@
         [jnp.stack([first_real, first_imag], axis=1), jnp.stack([second_real, second_imag], axis=1)]
     )
     convolved = inverse(spectrum, tables).astype(jnp.bfloat16)
-    token_rows = lax.all_to_all(convolved, "ctx", split_axis=2, concat_axis=1, tiled=True)
+    token_rows = jnp.concatenate(
+        lax.all_to_all(jnp.stack(jnp.split(convolved, lax.axis_size("ctx"), axis=2)), "ctx", 0, 0),
+        axis=1,
+    )
     mixed_b = token_rows[1][::-1]
     result = causal[0] * token_rows[0].astype(jnp.float32) + anticausal[0] * mixed_b.astype(
         jnp.float32

time: 103 us -> 97.2 us (0.944)
  local copies, waits for them, and re-layouts: 26.3 us -> 19.1 us
  other arithmetic: 20.2 us -> 21.8 us
    unnamed x67 -> x80, local copies, waits for them, and re-layouts: 19.2 us -> 13.5 us
    slice x1, other arithmetic: 0.07 us -> 1.66 us  [on_device(): mixed_b = token_rows[1][::-1]]
  transfers between devices with their start and end apart: 3 -> 3, of which waited for: 1 -> 1; matrix products, arithmetic and copies ran while one was open for 15% -> 16% of each run, Pallas kernels for 0% -> 0%
where the time goes in v1:
time: 97.2 us; the launch traced here: 96.8 us
  other arithmetic  21.8 us (22%)
  local copies, waits for them, and re-layouts  19.1 us (20%)
  blocking collectives  17.7 us (18%)
  matrix products  14.7 us (15%)
  starting transfers between devices  12.5 us (13%)
  waiting for transfers between devices  10.4 us (11%)
    all_to_all x1, blocking collectives, on_device(): lax.all_to_all(jnp.stack(jnp.split(convolved, lax.axis_size('ctx'), axis=...  17.7 us
    unnamed x80, local copies, waits for them, and re-layouts  13.5 us
    all_to_all x1, waiting for transfers between devices, on_device(): lax.all_to_all(outgoing, 'ctx', split_axis=1, concat_axis=2, tiled=True)  10.4 us
    all_to_all x1, starting transfers between devices, on_device(): lax.all_to_all(outgoing, 'ctx', split_axis=1, concat_axis=2, tiled=True)  8.13 us
    dot_general x2, matrix products, forward(): jnp.einsum('...cfb,cdbk->...dfk', twist, inner_fwd, precision=precise)  6.97 us
    add x1, other arithmetic, on_device(): anticausal + mirrored_taps[:, :, offset, None] * padded[:, :, later:later...  4.54 us
    dot_general x1, matrix products, inverse(): jnp.einsum('...cfk,cdkb->...dfb', spectrum, inner_inv, precision=precise)  4.47 us
    add x1, other arithmetic, on_device(): causal + short_taps[:, :, offset, None] * padded[:, :, begin:begin + tokens]  4.31 us
  transfers between devices with their start and end apart: 3, of which 1 were waited for; matrix products, arithmetic and copies ran while one was open for 16% of the time, Pallas kernels for 0%

profile of v1, /device:TPU:0, one launch (start us, length us, event | category | flops | bytes accessed | tf_op | source)
XLA Modules:
  0.0 96.8 jit_solution(13929710109463091467)
XLA Ops:
  0.0 1.3 %pad_maximum_fusion.2 = bf16[3,960,128]{2,1,0:T(8,128)(2,1)S(1)} fusion(bf16[1,960,128]{2,1,0:T(8,128)(2,1)} %bitcast.246, bf16[1,960,128]{2,1,0:T(8,128)(2,1)} %bitcast.250, bf16[1,960,128]{2,1,0:T(8,128)(2,1)} %bitcast.254), kind=kLoop, calls=%fused_computation.55 | loop fusion | flops 737280 | bytes 1474560 | tf_op jit(solution)/shard_map/stack | solution.py:80
  1.9 1.3 %collective-permute-start.1 = (bf16[3,960,6]{1,2,0:T(8,128)(2,1)S(1)}, bf16[3,960,6]{1,2,0:T(8,128)(2,1)S(1)}, u32[]{:S(2)}, u32[]{:S(2)}) collective-permute-start(bf16[3,960,6]{1,2,0:T(8,128)(2,1)S(1)} %copy.29), channel_id=1, source_target_pairs={{1,0},{2,1},{3,2},{4,3},{5,4},{6,5},{7,6},{8,7},{9,8},{10,9},{11,1... | collective-permute-start | bytes 103688 | tf_op jit(solution)/shard_map/ppermute | solution.py:19
  3.5 3.0 %collective-permute-start = (bf16[3,960,6]{1,2,0:T(8,128)(2,1)S(1)}, bf16[3,960,6]{1,2,0:T(8,128)(2,1)S(1)}, u32[]{:S(2)}, u32[]{:S(2)}) collective-permute-start(bf16[3,960,6]{1,2,0:T(8,128)(2,1)S(1)} %copy.25), channel_id=1, source_target_pairs={{0,1},{1,2},{2,3},{3,4},{4,5},{5,6},{6,7},{7,8},{8,9},{9,10},{10,1... | collective-permute-start | bytes 103688 | tf_op jit(solution)/shard_map/ppermute | solution.py:18
  7.3 0.7 reverse.8
  8.1 0.7 reverse.7
  9.0 0.7 reverse.12
  10.4 0.7 reverse.11
  11.2 0.7 reverse.10
  12.7 0.7 reverse.9
  14.1 0.6 copy_bitcast_fusion.20
  15.4 0.7 fusion.60
  16.7 0.7 reverse.13
  18.7 1.2 %copy.30 = bf16[3,960,6]{2,1,0:T(8,128)(2,1)} copy(bf16[3,960,6]{1,2,0:T(8,128)(2,1)S(1)} %collective-permute-done.1) | data formatting | bytes 69120 | tf_op jit(solution)/shard_map/ppermute | solution.py:19
  19.9 2.5 %maximum_maximum_fusion = (bf16[3,960,134]{2,1,0:T(8,128)(2,1)S(1)}, bf16[3,960,134]{2,1,0:T(8,128)(2,1)S(1)}) fusion(bf16[1,960,128]{2,1,0:T(8,128)(2,1)S(1)} %bitcast.247, bf16[1,960,128]{2,1,0:T(8,128)(2,1)S(1)} %bitcast.251, bf16[1,960,128]{2,1,0:T(8,128)(2,1)S(1)} %bitcast.255, bf16[3,960,6]{2,1,0:T(8,128)(2,1)S(1)} %copy.26, bf16[3,960,6]{2,1,0:T(8,128)(2,1)} %copy.30), kind=kLoop, calls=%fused_computation.39 | loop fusion | flops 6174720 | bytes 2350080 | tf_op jit(solution)/shard_map/concatenate | solution.py:20
  22.6 4.5 %fusion.31 = f32[3,960,128]{2,1,0:T(8,128)S(1)} fusion(bf16[3,960,134]{2,1,0:T(8,128)(2,1)S(1)} %get-tuple-element.16, f32[3,960]{1,0:T(4,128)S(1)} %copy-done.13, f32[3,960]{1,0:T(4,128)S(1)} %copy-done.14, f32[3,960]{1,0:T(4,128)S(1)} %copy-done.17, f32[3,960]{1,0:T(4,128)S(1)} %copy-done.18, f32[3,960]{1,0:T(4,128)S(1)} %copy-done.15, ...), kind=kLoop, calls=%fused_computation.38 | loop fusion | flops 8110080 | bytes 6716160 | tf_op jit(solution)/shard_map/add | solution.py:90
  27.1 1.1 %copy-done = f32[3,960,128]{2,1,0:T(8,128)} copy-done((f32[3,960,128]{2,1,0:T(8,128)}, f32[3,960,128]{2,1,0:T(8,128)S(1)}, u32[]{:S(2)}) %copy-start) | copy-done | bytes 1474584
  29.0 4.3 %fusion.25 = f32[3,960,128]{2,1,0:T(8,128)S(1)} fusion(bf16[3,960,134]{2,1,0:T(8,128)(2,1)S(1)} %get-tuple-element.15, f32[3,960]{1,0:T(4,128)S(1)} %get-tuple-element.50, f32[3,960]{1,0:T(4,128)S(1)} %get-tuple-element.51, f32[3,960]{1,0:T(4,128)S(1)} %copy-done.11, f32[3,960]{1,0:T(4,128)S(1)} %copy-done.12, f32[3,960]{1,0:T(4,128)S(1)} %copy-done.9, ...), kind=kLoop, calls=%fused_computation.32 | loop fusion | flops 8110080 | bytes 6716160 | tf_op jit(solution)/shard_map/add | solution.py:87
  33.3 1.1 %copy-done.1 = f32[3,960,128]{2,1,0:T(8,128)} copy-done((f32[3,960,128]{2,1,0:T(8,128)}, f32[3,960,128]{2,1,0:T(8,128)S(1)}, u32[]{:S(2)}) %copy-start.1) | copy-done | bytes 1474584
  34.5 1.3 %copy.31 = bf16[2,960,128]{2,0,1:T(2,128)(2,1)} copy(bf16[2,960,128]{2,1,0:T(8,128)(2,1)S(1)} %pad_maximum_fusion.3) | data formatting | bytes 983040 | tf_op jit(solution)/shard_map/stack | solution.py:95
  35.8 8.1 %all-to-all-start = ((bf16[2,960,128]{2,0,1:T(2,128)(2,1)}), bf16[2,960,128]{2,0,1:T(2,128)(2,1)S(1)}, u32[]{:S(2)}, u32[]{:S(2)}) async-start(bf16[2,960,128]{2,0,1:T(2,128)(2,1)} %copy.31), calls=%async_computation | async-start | bytes 983040 | tf_op jit(solution)/shard_map/all_to_all | solution.py:96
  44.0 0.7 convolution_bitcast_fusion.1
  45.2 2.0 %fusion.17 = f32[60,2,32,128]{3,0,2,1:T(8,128)S(1)} fusion(f32[60,2,32,128]{3,2,0,1:T(8,128)S(1)} %pad_maximum_fusion, f32[1,2,128,128]{3,2,0,1:T(8,128)S(1)} %get-tuple-element.38, f32[1,2,128,128]{3,2,0,1:T(8,128)S(1)} %get-tuple-element.48), kind=kOutput, calls=%fused_computation.25 | convolution fusion | flops 755040256 | bytes 4194304 | tf_op jit(solution)/shard_map/...cfb,cdbk->...dfk/dot_general | solution.py:57
  47.2 10.4 %all-to-all-done = bf16[2,960,128]{2,0,1:T(2,128)(2,1)S(1)} async-done(((bf16[2,960,128]{2,0,1:T(2,128)(2,1)}), bf16[2,960,128]{2,0,1:T(2,128)(2,1)S(1)}, u32[]{:S(2)}, u32[]{:S(2)}) %all-to-all-start) | async-done | bytes 491552 | tf_op jit(solution)/shard_map/all_to_all | solution.py:96
  57.6 1.2 %convolution_bitcast_fusion = f32[2,60,2,32,128]{4,3,1,0,2:T(8,128)S(1)} fusion(bf16[2,16,60,128]{3,0,2,1:T(2,128)(2,1)S(1)} %bitcast.258, f32[1,16,32]{2,1,0:T(8,128)S(1)} %get-tuple-element.62, f32[1,16,32]{2,1,0:T(8,128)S(1)} %get-tuple-element.63), kind=kOutput, calls=%fused_computation.17 | convolution fusion | flops 94372864 | bytes 4427776 | tf_op jit(solution)/shard_map/...ab,caf->...cfb/dot_general | solution.py:47
  58.8 0.8 multiply_add_fusion.1
  60.0 5.0 %fusion.8 = f32[2,60,2,32,128]{4,1,3,2,0:T(8,128)S(1)} fusion(f32[2,60,2,32,128,1]{4,3,1,0,2,5:T(8,128)S(1)} %maximum_bitcast_fusion.1, f32[1,2,128,128]{3,2,0,1:T(8,128)S(1)} %get-tuple-element.38, f32[1,2,128,128]{3,2,0,1:T(8,128)S(1)} %get-tuple-element.48), kind=kOutput, calls=%fused_computation.10 | convolution fusion | flops 1510014976 | bytes 8126464 | tf_op jit(solution)/shard_map/...cfb,cdbk->...dfk/dot_general | solution.py:57
  65.0 1.0 multiply_subtract_fusion.3
  67.3 4.5 %fusion.14 = f32[2,60,2,32,128]{4,3,1,0,2:T(8,128)S(1)} fusion(f32[2,60,2,32,128,1]{4,1,3,2,0,5:T(8,128)S(1)} %maximum_bitcast_fusion, f32[1,2,128,128]{3,2,1,0:T(8,128)S(1)} %copy-done.7, f32[1,2,128,128]{3,2,1,0:T(8,128)S(1)} %copy-done.6), kind=kOutput, calls=%fused_computation.16 | convolution fusion | flops 1510014976 | bytes 8126464 | tf_op jit(solution)/shard_map/...cfk,cdkb->...dfb/dot_general | solution.py:62
  72.4 1.3 %fusion.41 = bf16[2,60,16,128]{3,2,1,0:T(8,128)(2,1)S(1)} fusion(f32[2,60,1,32,128]{4,3,1,0,2:T(8,128)S(1)} %get-tuple-element.10, f32[2,60,1,32,128]{4,3,1,0,2:T(8,128)S(1)} %get-tuple-element.9, f32[1,16,32]{2,1,0:T(8,128)S(1)} %get-tuple-element.62, f32[1,16,32]{2,1,0:T(8,128)S(1)} %get-tuple-element.63), kind=kOutput, calls=%fused_computation.44 | convolution fusion | flops 95847424 | bytes 4427776 | tf_op jit(solution)/shard_map/...cfb,caf->...ab/dot_general | solution.py:72
  74.8 17.7 %all_to_all.20 = bf16[16,2,60,128]{3,1,2,0:T(2,128)(2,1)S(1)} all-to-all(bf16[16,2,60,128]{3,1,2,0:T(2,128)(2,1)S(1)} %constant_dynamic-update-slice_fusion), channel_id=1, replica_groups=mesh['grp'=2,'ctx'=16] {'ctx'}, dimensions={0} | all-to-all | bytes 983040 | tf_op jit(solution)/shard_map/all_to_all | solution.py:112
  92.5 1.7 %slice_reduce_fusion = (bf16[16,60,128]{2,1,0:T(8,128)(2,1)S(1)}, f32[1,16,60,128]{3,0,2,1:T(1,128)S(1)}) fusion(bf16[2,16,60,128]{3,0,2,1:T(2,128)(2,1)S(1)} %bitcast.245), kind=kLoop, calls=%fused_computation.56 | loop fusion | flops 122880 | bytes 1228800 | tf_op jit(solution)/shard_map/slice | solution.py:115
  94.8 2.0 %fusion.46 = bf16[960,128]{1,0:T(8,128)(2,1)} fusion(f32[3,960,128]{2,1,0:T(8,128)} %copy-done, f32[960,128]{1,0:T(8,128)S(1)} %bitcast.259, f32[3,960,128]{2,1,0:T(8,128)} %copy-done.1, bf16[960,128]{1,0:T(8,128)(2,1)S(1)} %rev.8), kind=kLoop, calls=%fused_computation.60 | loop fusion | flops 614400 | bytes 1966080 | tf_op jit(solution)/shard_map/convert_element_type | solution.py:119
  (97 shorter events, 11.7 us)
Async XLA Ops:
  1.3 5.9 %copy-start.8 = (f32[3,960,7]{1,2,0:T(8,128)S(1)}, f32[3,960,7]{1,2,0:T(8,128)}, u32[]{:S(2)}) copy-start(f32[3,960,7]{1,2,0:T(8,128)} %param.8) | copy-start | bytes 241924
  1.6 16.6 %copy-start.5 = (bf16[60,2048]{1,0:T(8,128)(2,1)S(1)}, bf16[60,2048]{1,0:T(8,128)(2,1)}, u32[]{:S(2)}) copy-start(bf16[60,2048]{1,0:T(8,128)(2,1)} %param.9) | copy-start | bytes 737284
  1.9 16.8 %collective-permute-start.1 = (bf16[3,960,6]{1,2,0:T(8,128)(2,1)S(1)}, bf16[3,960,6]{1,2,0:T(8,128)(2,1)S(1)}, u32[]{:S(2)}, u32[]{:S(2)}) collective-permute-start(bf16[3,960,6]{1,2,0:T(8,128)(2,1)S(1)} %copy.29), channel_id=1, source_target_pairs={{1,0},{2,1},{3,2},{4,3},{5,4},{6,5},{7,6},{8,7},{9,8},{10,9},{11,1... | collective-permute-start | bytes 103688 | tf_op jit(solution)/shard_map/ppermute | solution.py:19
  3.5 14.7 %collective-permute-start = (bf16[3,960,6]{1,2,0:T(8,128)(2,1)S(1)}, bf16[3,960,6]{1,2,0:T(8,128)(2,1)S(1)}, u32[]{:S(2)}, u32[]{:S(2)}) collective-permute-start(bf16[3,960,6]{1,2,0:T(8,128)(2,1)S(1)} %copy.25), channel_id=1, source_target_pairs={{0,1},{1,2},{2,3},{3,4},{4,5},{5,6},{6,7},{7,8},{8,9},{9,10},{10,1... | collective-permute-start | bytes 103688 | tf_op jit(solution)/shard_map/ppermute | solution.py:18
  6.9 13.0 %copy-start.2 = (bf16[960,128]{1,0:T(8,128)(2,1)S(1)}, bf16[960,128]{1,0:T(8,128)(2,1)}, u32[]{:S(2)}) copy-start(bf16[960,128]{1,0:T(8,128)(2,1)} %param.7) | copy-start | bytes 737284
  6.9 13.0 %copy-start.3 = (bf16[960,128]{1,0:T(8,128)(2,1)S(1)}, bf16[960,128]{1,0:T(8,128)(2,1)}, u32[]{:S(2)}) copy-start(bf16[960,128]{1,0:T(8,128)(2,1)} %param.6) | copy-start | bytes 737284
  6.9 13.0 %copy-start.4 = (bf16[960,128]{1,0:T(8,128)(2,1)S(1)}, bf16[960,128]{1,0:T(8,128)(2,1)}, u32[]{:S(2)}) copy-start(bf16[960,128]{1,0:T(8,128)(2,1)} %param.5) | copy-start | bytes 737284
  19.9 2.6 %copy-start.13 = (f32[3,960]{1,0:T(4,128)S(1)}, f32[3,960]{1,0:T(4,128)}, u32[]{:S(2)}) copy-start(f32[3,960]{1,0:T(4,128)} %get-tuple-element.56) | copy-start | bytes 34564
  19.9 2.6 %copy-start.14 = (f32[3,960]{1,0:T(4,128)S(1)}, f32[3,960]{1,0:T(4,128)}, u32[]{:S(2)}) copy-start(f32[3,960]{1,0:T(4,128)} %get-tuple-element.57) | copy-start | bytes 34564
  19.9 2.6 %copy-start.15 = (f32[3,960]{1,0:T(4,128)S(1)}, f32[3,960]{1,0:T(4,128)}, u32[]{:S(2)}) copy-start(f32[3,960]{1,0:T(4,128)} %get-tuple-element.60) | copy-start | bytes 34564
  19.9 2.6 %copy-start.16 = (f32[3,960]{1,0:T(4,128)S(1)}, f32[3,960]{1,0:T(4,128)}, u32[]{:S(2)}) copy-start(f32[3,960]{1,0:T(4,128)} %get-tuple-element.61) | copy-start | bytes 34564
  19.9 2.6 %copy-start.17 = (f32[3,960]{1,0:T(4,128)S(1)}, f32[3,960]{1,0:T(4,128)}, u32[]{:S(2)}) copy-start(f32[3,960]{1,0:T(4,128)} %get-tuple-element.58) | copy-start | bytes 34564
  19.9 2.6 %copy-start.18 = (f32[3,960]{1,0:T(4,128)S(1)}, f32[3,960]{1,0:T(4,128)}, u32[]{:S(2)}) copy-start(f32[3,960]{1,0:T(4,128)} %get-tuple-element.59) | copy-start | bytes 34564
  19.9 2.6 %copy-start.20 = (f32[3,960,1]{1,0,2:T(4,128)S(1)}, f32[3,960,1]{1,0,2:T(4,128)}, u32[]{:S(2)}) copy-start(f32[3,960,1]{1,0,2:T(4,128)} %copy.175) | copy-start | bytes 34564
  22.5 6.4 %copy-start.9 = (f32[3,960]{1,0:T(4,128)S(1)}, f32[3,960]{1,0:T(4,128)}, u32[]{:S(2)}) copy-start(f32[3,960]{1,0:T(4,128)} %get-tuple-element.54) | copy-start | bytes 34564
  22.5 6.4 %copy-start.10 = (f32[3,960]{1,0:T(4,128)S(1)}, f32[3,960]{1,0:T(4,128)}, u32[]{:S(2)}) copy-start(f32[3,960]{1,0:T(4,128)} %get-tuple-element.55) | copy-start | bytes 34564
  22.6 6.4 %copy-start.11 = (f32[3,960]{1,0:T(4,128)S(1)}, f32[3,960]{1,0:T(4,128)}, u32[]{:S(2)}) copy-start(f32[3,960]{1,0:T(4,128)} %get-tuple-element.52) | copy-start | bytes 34564
  22.6 6.4 %copy-start.12 = (f32[3,960]{1,0:T(4,128)S(1)}, f32[3,960]{1,0:T(4,128)}, u32[]{:S(2)}) copy-start(f32[3,960]{1,0:T(4,128)} %get-tuple-element.53) | copy-start | bytes 34564
  22.6 6.4 %copy-start.19 = (f32[3,960,1]{1,0,2:T(4,128)S(1)}, f32[3,960,1]{1,0,2:T(4,128)}, u32[]{:S(2)}) copy-start(f32[3,960,1]{1,0,2:T(4,128)} %copy.176) | copy-start | bytes 34564
  27.1 1.1 %copy-start = (f32[3,960,128]{2,1,0:T(8,128)}, f32[3,960,128]{2,1,0:T(8,128)S(1)}, u32[]{:S(2)}) copy-start(f32[3,960,128]{2,1,0:T(8,128)S(1)} %fusion.31) | copy-start | bytes 4423684
  33.3 1.1 %copy-start.1 = (f32[3,960,128]{2,1,0:T(8,128)}, f32[3,960,128]{2,1,0:T(8,128)S(1)}, u32[]{:S(2)}) copy-start(f32[3,960,128]{2,1,0:T(8,128)S(1)} %fusion.25) | copy-start | bytes 4423684
  35.8 21.7 %all-to-all-start = ((bf16[2,960,128]{2,0,1:T(2,128)(2,1)}), bf16[2,960,128]{2,0,1:T(2,128)(2,1)S(1)}, u32[]{:S(2)}, u32[]{:S(2)}) async-start(bf16[2,960,128]{2,0,1:T(2,128)(2,1)} %copy.31), calls=%async_computation | async-start | bytes 983040 | tf_op jit(solution)/shard_map/all_to_all | solution.py:96
  66.3 0.9 copy-start.6
  66.4 1.0 copy-start.7
